TPU v7x, 512 devices: a whole 4x4x16 slice. The times are simulated.
512 devices in a mesh: pairs: 128 (over x, z, core), ints: 4 (over y).
Axes of the slice: x: 4, y: 4, z: 16, core: 2. Of those that a mesh axis runs over, the one named last changes fastest.
Arguments:
- amps: float32 [256, 256, 256], P('pairs', 'ints'), may hold values from -0.8 to 0.8
- resid_rest: float32 [256, 256, 256], P('pairs', 'ints'), may hold values from -6 to 6
- int_blocks: bfloat16 [128, 256, 256], P('pairs'), may hold values from -0.375 to 0.375
- virt_energy: float32 [256, 256], P('pairs'), may hold values from 0.5 to 3
- pair_energy: float32 [256], P('pairs'), may hold values from -2 to -0.5
- item_block: int32 [32768, 1], P(('pairs', 'ints')), may hold values from 0 to 127; in each aligned block of 64 rows (0 to 63, 64 to 127, ...) at most 2 rows name the same one
- share_owner: int32 [12288, 1], P('pairs'), may hold values from 0 to 127; in each aligned block of 96 rows (0 to 95, 96 to 191, ...) at most 2 rows name the same one
- share_pair: int32 [12288, 1], P('pairs'), may hold values from 0 to 1
- share_amp: int32 [12288, 1], P('pairs'), may hold values from 0 to 1
- transpose_pair: int32 [256], P('pairs'), may hold values from 0 to 255, as said below
Outputs:
- update: float32 [256, 256, 256], P('pairs', 'ints')
Inputs may be any that keep to these rules, and one draw needn't show every extreme that they name: `item_block`: within each aligned block of 64 rows no value occurs more than 2 times, and some value occurs exactly 2 times. `share_owner`: within each aligned block of 96 rows no value occurs more than 2 times, and some value occurs exactly 2 times. `transpose_pair`: A permutation equal to its own inverse; pair p maps into the block of 2 consecutive pairs whose block number is (p // 2 + 256 // 4) modulo 256 // 2.
All inputs are finite; a program needn't handle non-finite values.
Results may differ from a plain program's by a relative error of at most 0.008.
Values may be sent and summed in bfloat16 or wider, within the bound.
A program may use at most 64 MiB of HBM per device.

v0:
```python
import jax
import jax.numpy as jnp
from jax import lax
from jax.sharding import Mesh
from jax.sharding import PartitionSpec as P

PAIRS = ("pairs_0", "pairs_1", "pairs_2")
PAIRS_INTS = ("pairs_0", "pairs_1", "pairs_2", "ints")


def in_blocks(array, dim, size):
    before, after = (array.shape[:dim], array.shape[dim + 1 :])
    return jnp.moveaxis(array.reshape(*before, size, -1, *after), dim, 0)


def sum_at_owner(array, axis, dim):
    tiles = in_blocks(array, dim, lax.axis_size(axis))
    arrived = lax.all_to_all(tiles, axis, split_axis=0, concat_axis=0, tiled=True)
    return arrived.astype(jnp.float32).sum(axis=0)


def laid_out(tiles, dim):
    dims = list(tiles.shape[1:])
    dims[dim] *= tiles.shape[0]
    return jnp.moveaxis(tiles, 0, dim).reshape(dims)


def stacked_from(array, axes, order):
    tiles = array
    for k in order:
        tiles = lax.all_gather(tiles, axes[k])
    done = order[::-1]
    back = [done.index(k) for k in range(len(axes))]
    tiles = tiles.transpose(*back, *range(len(axes), tiles.ndim))
    return tiles.reshape(-1, *array.shape)


def gather_axes(array, axes, order, dim):
    return laid_out(stacked_from(array, axes, order), dim)


def from_behind(value, axis, steps):
    count = lax.axis_size(axis)
    pairs = [(source, (source + steps) % count) for source in range(count)]
    return lax.ppermute(value, axis, pairs)


def slot_ranks(targets, n_groups):
    match_hits = (targets[:, None] == jnp.arange(n_groups, dtype=jnp.int32)[None, :]).astype(
        jnp.int32
    )
    before = jnp.cumsum(match_hits, axis=0) - match_hits
    return jnp.sum(before * match_hits, axis=1)


def body(
    amps,
    resid_rest,
    int_blocks,
    virt_energy,
    pair_energy,
    item_block,
    share_owner,
    share_pair,
    share_amp,
    transpose_pair,
):
    n_pairs = lax.axis_size(PAIRS)
    pair_index = lax.axis_index(PAIRS)
    quarter = lax.axis_index("ints")
    pair_count, row_count, domain = amps.shape
    amp_half = amps.astype(jnp.bfloat16)
    n_items = item_block.shape[0]
    item_height = pair_count * row_count // n_items
    item_rows = amp_half.reshape(n_items, item_height, domain)
    block_targets = item_block[:, 0]
    cap_items = max(2, 3 * n_items // (2 * n_pairs))
    item_slot = block_targets * cap_items + slot_ranks(block_targets, n_pairs)
    outgoing = (
        jnp.zeros((n_pairs * cap_items, item_height, domain), jnp.bfloat16)
        .at[item_slot]
        .set(item_rows)
    )
    outgoing = outgoing.reshape(n_pairs, cap_items, item_height, domain)
    resident = int_blocks[0]
    arrived = lax.all_to_all(outgoing, PAIRS, split_axis=0, concat_axis=0, tiled=True)
    leading = arrived.shape[:3]
    product = jnp.dot(arrived.reshape(-1, domain), resident, preferred_element_type=jnp.float32)
    product = product.astype(jnp.bfloat16).reshape(leading + (domain,))
    returned = lax.all_to_all(product, PAIRS, split_axis=0, concat_axis=0, tiled=True)
    x_rows = returned.reshape(n_pairs * cap_items, item_height, domain)[item_slot]
    x_rows = x_rows.reshape(pair_count, row_count, domain)
    partial_value = jnp.einsum("pac,pad->pcd", amp_half, x_rows, preferred_element_type=jnp.float32)
    intermed = sum_at_owner(partial_value.astype(jnp.bfloat16), "ints", 1).astype(jnp.bfloat16)
    amp_full = lax.all_gather(amp_half, "ints", axis=1, tiled=True)
    owners = share_owner[:, 0]
    wanted = share_pair[:, 0]
    n_req = owners.shape[0]
    per_pair = n_req // pair_count
    source_global = owners * pair_count + wanted
    empty_rows = jnp.zeros((n_req, row_count, domain), jnp.bfloat16)
    piece = gather_axes(intermed, PAIRS, (0, 1, 2), 0)
    start = jnp.int32(0)
    local = jnp.clip(source_global, 0, piece.shape[0] - 1)
    inside = (source_global >= start) & (source_global < start + piece.shape[0])
    picked = jnp.where(inside[:, None, None], piece[local], empty_rows)
    picked = picked.reshape(pair_count, per_pair, row_count, domain)
    partners = share_amp[:, 0].reshape(pair_count, per_pair)

    def cycle_one(packed):
        w_req, amp_index = packed
        return jnp.einsum(
            "kac,kcb->ab", w_req, amp_full[amp_index], preferred_element_type=jnp.float32
        )

    cycle_term = lax.map(cycle_one, (picked, partners))
    energies_rows = lax.dynamic_slice_in_dim(virt_energy, quarter * row_count, row_count, 1)
    divisor = energies_rows[:, :, None] + virt_energy[:, None, :] - pair_energy[:, None, None]
    scaled = (resid_rest + cycle_term) / divisor
    mirror_part = from_behind(scaled.astype(jnp.bfloat16), PAIRS, n_pairs // 2).astype(scaled.dtype)
    turned = lax.all_to_all(
        mirror_part.astype(jnp.bfloat16), "ints", split_axis=2, concat_axis=1, tiled=True
    ).astype(mirror_part.dtype)
    partner_dev = (pair_index + n_pairs // 2) % n_pairs
    local_swap = transpose_pair - partner_dev * pair_count
    mirrored = jnp.transpose(turned[local_swap], (0, 2, 1))
    return -0.5 * (scaled + mirrored)


def solution(mesh):
    torus = Mesh(
        mesh.devices.reshape(4, 16, 2, mesh.shape["ints"]),
        ("pairs_0", "pairs_1", "pairs_2", "ints"),
    )
    return jax.shard_map(
        body,
        mesh=torus,
        in_specs=(
            P(PAIRS, "ints", None),
            P(PAIRS, "ints", None),
            P(PAIRS, None, None),
            P(PAIRS, None),
            P(PAIRS),
            P(PAIRS_INTS, None),
            P(PAIRS, None),
            P(PAIRS, None),
            P(PAIRS, None),
            P(PAIRS),
        ),
        out_specs=P(PAIRS, "ints", None),
        check_vma=False,
    )
```

profile of v0, /device:TPU:2, one launch (start us, length us, event | category | flops | bytes accessed | tf_op | source)
XLA Modules:
  0.0 273.0 jit_solution(6148034309779576829)
XLA Ops:
  8.9 0.9 convert_element_type.35
  10.0 2.4 scatter_fusion
  12.4 42.1 %all_to_all.24 = bf16[128,2,2,256]{3,2,1,0:T(2,128)(2,1)S(1)} all-to-all(bf16[128,2,2,256]{3,2,1,0:T(2,128)(2,1)S(1)} %bitcast.79), channel_id=1, replica_groups=mesh['pairs_0'=4,'pairs_1'=16,'pairs_2'=2,'ints'=4] {'pairs_0','pairs_1'..., dimensions={0} | all-to-all | bytes 524288 | tf_op jit(solution)/shard_map/all_to_all | solution.py:86
  55.6 7.1 %all-to-all-start.1 = ((bf16[128,2,2,256]{3,2,1,0:T(2,128)(2,1)}), bf16[128,2,2,256]{3,2,1,0:T(2,128)(2,1)S(1)}, u32[]{:S(2)}, u32[]{:S(2)}) async-start(bf16[128,2,2,256]{3,2,1,0:T(2,128)(2,1)} %reshape.85), calls=%async_computation.1 | async-start | bytes 524288 | tf_op jit(solution)/shard_map/all_to_all | solution.py:90
  62.8 22.7 %all-to-all-done.1 = bf16[128,2,2,256]{3,2,1,0:T(2,128)(2,1)S(1)} async-done(((bf16[128,2,2,256]{3,2,1,0:T(2,128)(2,1)}), bf16[128,2,2,256]{3,2,1,0:T(2,128)(2,1)S(1)}, u32[]{:S(2)}, u32[]{:S(2)}) %all-to-all-start.1) | async-done | bytes 262176 | tf_op jit(solution)/shard_map/all_to_all | solution.py:90
  86.6 11.0 %all_to_all.25 = bf16[4,2,64,256]{3,2,1,0:T(8,128)(2,1)S(1)} all-to-all(bf16[4,2,64,256]{3,2,1,0:T(8,128)(2,1)S(1)} %bitcast.83), channel_id=1, replica_groups=mesh['pairs_0'=4,'pairs_1'=16,'pairs_2'=2,'ints'=4] {'ints'}, dimensions={0} | all-to-all | bytes 524288 | tf_op jit(solution)/shard_map/all_to_all | solution.py:18
  97.6 12.2 %all-gather = bf16[8,64,256]{2,1,0:T(8,128)(2,1)} all-gather(bf16[2,64,256]{2,1,0:T(8,128)(2,1)S(1)} %reduce_sum.25), channel_id=2, replica_groups=mesh['pairs_0'=4,'pairs_1'=16,'pairs_2'=2,'ints'=4] {'pairs_0'}, dimensions={0}, use_global_device_ids=true | all-gather | bytes 327680 | tf_op jit(solution)/shard_map/all_gather | solution.py:31
  109.9 68.5 %all-gather.6.cloned.1.call-done = bf16[64,2,64,256]{3,2,1,0:T(8,128)(2,1)} async-done(((bf16[4,2,64,256]{3,2,1,0:T(8,128)(2,1)}), bf16[64,2,64,256]{3,2,1,0:T(8,128)(2,1)}) %all-gather.6.cloned.1.call-update) | async-done | bytes 4194320 | tf_op jit(solution)/shard_map/all_gather | solution.py:31
  180.4 12.6 %all_gather.27 = bf16[2,256,256]{2,1,0:T(8,128)(2,1)S(1)} all-gather(bf16[2,64,256]{2,1,0:T(8,128)(2,1)S(1)} %convert_element_type.35), channel_id=1, replica_groups=mesh['pairs_0'=4,'pairs_1'=16,'pairs_2'=2,'ints'=4] {'ints'}, dimensions={1}, use_global_device_ids=true | all-gather | bytes 327680 | tf_op jit(solution)/shard_map/all_gather | solution.py:95
  193.0 14.2 %all-gather.8.cloned.1.call-done = bf16[32,4,2,64,256]{4,3,2,1,0:T(8,128)(2,1)} async-done(((bf16[16,4,2,64,256]{4,3,2,1,0:T(8,128)(2,1)}), bf16[32,4,2,64,256]{4,3,2,1,0:T(8,128)(2,1)}) %all-gather.8.cloned.1.call-update) | async-done | bytes 8388624 | tf_op jit(solution)/shard_map/all_gather | solution.py:31
  207.2 8.3 %copy.15 = bf16[4,16,2,2,64,256]{5,4,3,2,1,0:T(8,128)(2,1)} copy(bf16[4,16,2,2,64,256]{5,4,3,0,1,2:T(8,128)(2,1)} %bitcast.77) | data formatting | bytes 16777216 | tf_op jit(solution)/shard_map/transpose | solution.py:34
  215.4 5.9 %gather_fusion.2 = bf16[96,64,256]{2,1,0:T(8,128)(2,1)} fusion(bf16[256,64,256]{2,1,0:T(8,128)(2,1)} %bitcast.75, s32[1024]{0:T(1024)S(1)} %pad_clamp_fusion.2), kind=kCustom, calls=%fused_computation.2 | custom fusion | bytes 6291840 | tf_op jit(solution)/shard_map/gather | solution.py:106
  221.4 2.2 broadcast_select_fusion
  223.6 20.3 %while.10 = (s32[]{:T(128)}, f32[2,64,256]{2,1,0:T(8,128)}, bf16[2,48,64,256]{3,2,1,0:T(8,128)(2,1)S(1)}, s32[2,48]{1,0:T(2,128)}, bf16[2,256,256]{2,1,0:T(8,128)(2,1)S(1)}, /*index=5*/s32[]{:T(128)}) while((s32[]{:T(128)}, f32[2,64,256]{2,1,0:T(8,128)}, bf16[2,48,64,256]{3,2,1,0:T(8,128)(2,1)S(1)}, s32[2,48]{1,0:T(2,128)}, ...), condition=%wide.region_5.6_spmd, body=%wide.region_4.5_spmd.sunk | while | flops 402654368 | bytes 20518728 | solution.py:116
  224.2 4.9 %gather_fusion = bf16[48,256,256]{2,1,0:T(8,128)(2,1)} fusion(bf16[2,256,256]{2,1,0:T(8,128)(2,1)S(1)} %get-tuple-element.90, s32[1024]{0:T(1024)S(1)} %pad_clamp_fusion.5), kind=kCustom, calls=%fused_computation.clone.1 | custom fusion | bytes 12583104 | tf_op jit(solution)/shard_map/while/body/eval_jaxpr/gather | solution.py:113
  229.1 4.6 %fusion.29 = f32[2,64,256]{2,1,0:T(8,128)} fusion(f32[2,64,256]{2,1,0:T(8,128)} %get-tuple-element.81, s32[]{:T(128)} %get-tuple-element.80, bf16[48,256,256]{2,1,0:T(8,128)(2,1)} %gather_fusion, bf16[2,48,64,256]{3,2,1,0:T(8,128)(2,1)S(1)} %get-tuple-element.88), kind=kOutput, calls=%fused_computation.9.clone.1 | convolution fusion | flops 402653184 | bytes 7930880 | tf_op jit(solution)/shard_map/while/body/eval_jaxpr/kac,kcb->ab/dot_general | solution.py:112
  234.4 4.8 %gather_fusion = bf16[48,256,256]{2,1,0:T(8,128)(2,1)} fusion(bf16[2,256,256]{2,1,0:T(8,128)(2,1)S(1)} %get-tuple-element.90, s32[1024]{0:T(1024)S(1)} %pad_clamp_fusion.5), kind=kCustom, calls=%fused_computation.clone.1 | custom fusion | bytes 12583104 | tf_op jit(solution)/shard_map/while/body/eval_jaxpr/gather | solution.py:113
  239.2 4.6 %fusion.29 = f32[2,64,256]{2,1,0:T(8,128)} fusion(f32[2,64,256]{2,1,0:T(8,128)} %get-tuple-element.81, s32[]{:T(128)} %get-tuple-element.80, bf16[48,256,256]{2,1,0:T(8,128)(2,1)} %gather_fusion, bf16[2,48,64,256]{3,2,1,0:T(8,128)(2,1)S(1)} %get-tuple-element.88), kind=kOutput, calls=%fused_computation.9.clone.1 | convolution fusion | flops 402653184 | bytes 7930880 | tf_op jit(solution)/shard_map/while/body/eval_jaxpr/kac,kcb->ab/dot_general | solution.py:112
  243.8 1.1 fusion.17
  244.9 3.9 %collective-permute-start = (bf16[2,64,256]{2,1,0:T(8,128)(2,1)S(1)}, bf16[2,64,256]{2,1,0:T(8,128)(2,1)S(1)}, u32[]{:S(2)}, u32[]{:S(2)}) collective-permute-start(bf16[2,64,256]{2,1,0:T(8,128)(2,1)S(1)} %fusion.17), channel_id=1, source_target_pairs={{0,256},{4,260},{8,264},{12,268},{16,272},{20,276},{24,280},{28,28... | collective-permute-start | bytes 196616 | tf_op jit(solution)/shard_map/ppermute | solution.py:45
  249.5 3.1 %collective-permute-done = bf16[2,64,256]{2,1,0:T(8,128)(2,1)S(1)} collective-permute-done((bf16[2,64,256]{2,1,0:T(8,128)(2,1)S(1)}, bf16[2,64,256]{2,1,0:T(8,128)(2,1)S(1)}, u32[]{:S(2)}, u32[]{:S(2)}) %collective-permute-start) | collective-permute-done | bytes 65568 | tf_op jit(solution)/shard_map/ppermute | solution.py:45
  253.5 4.3 %all-to-all-start.3 = ((bf16[4,2,4096]{2,1,0:T(2,128)(2,1)}), bf16[4,2,4096]{2,1,0:T(2,128)(2,1)S(1)}, u32[]{:S(2)}, u32[]{:S(2)}) async-start(bf16[4,2,4096]{2,1,0:T(2,128)(2,1)} %reshape.152), calls=%async_computation.3 | async-start | bytes 131072 | tf_op jit(solution)/shard_map/all_to_all | solution.py:121
  257.8 5.6 %all-to-all-done.3 = bf16[4,2,4096]{2,1,0:T(2,128)(2,1)S(1)} async-done(((bf16[4,2,4096]{2,1,0:T(2,128)(2,1)}), bf16[4,2,4096]{2,1,0:T(2,128)(2,1)S(1)}, u32[]{:S(2)}, u32[]{:S(2)}) %all-to-all-start.3) | async-done | bytes 65568 | tf_op jit(solution)/shard_map/all_to_all | solution.py:121
  264.4 1.7 fusion.12
  (52 shorter events, 10.8 us)
Async XLA Ops:
  6.5 48.1 %copy-start = (bf16[1,256,256]{2,1,0:T(8,128)(2,1)S(1)}, bf16[1,256,256]{2,1,0:T(8,128)(2,1)}, u32[]{:S(2)}) copy-start(bf16[1,256,256]{2,1,0:T(8,128)(2,1)} %param.14) | copy-start | bytes 393220
  55.6 29.9 %all-to-all-start.1 = ((bf16[128,2,2,256]{3,2,1,0:T(2,128)(2,1)}), bf16[128,2,2,256]{3,2,1,0:T(2,128)(2,1)S(1)}, u32[]{:S(2)}, u32[]{:S(2)}) async-start(bf16[128,2,2,256]{3,2,1,0:T(2,128)(2,1)} %reshape.85), calls=%async_computation.1 | async-start | bytes 524288 | tf_op jit(solution)/shard_map/all_to_all | solution.py:90
  62.8 115.5 %all-gather.6.cloned.1.call-start = ((), (), s32[]{:S(2)}) async-start(), calls=%async_computation.4 | async-start | bytes 4456448 | tf_op jit(solution)/shard_map/all_gather | solution.py:31
  86.5 91.8 %copy-start.4 = (s32[96,1]{0,1:T(1,128)S(1)}, s32[96,1]{0,1:T(1,128)}, u32[]{:S(2)}) copy-start(s32[96,1]{0,1:T(1,128)} %param.19) | copy-start | bytes 1156
  86.5 91.8 %copy-start.5 = (s32[96,1]{0,1:T(1,128)S(1)}, s32[96,1]{0,1:T(1,128)}, u32[]{:S(2)}) copy-start(s32[96,1]{0,1:T(1,128)} %param.18) | copy-start | bytes 1156
  86.6 92.5 %copy-start.3 = (s32[96,1]{0,1:T(1,128)S(1)}, s32[96,1]{0,1:T(1,128)}, u32[]{:S(2)}) copy-start(s32[96,1]{0,1:T(1,128)} %param.20) | copy-start | bytes 1156
  86.6 106.3 %copy-start.1 = (f32[2,256]{1,0:T(2,128)S(1)}, f32[2,256]{1,0:T(2,128)}, u32[]{:S(2)}) copy-start(f32[2,256]{1,0:T(2,128)} %param.15) | copy-start | bytes 6148
  109.8 97.4 %all-gather.8.cloned.1.call-start = ((), (), s32[]{:S(2)}) async-start(), calls=%async_computation.5 | async-start | bytes 12582912 | tf_op jit(solution)/shard_map/all_gather | solution.py:31
  223.6 20.3 %copy-start.2 = (f32[2]{0:T(128)S(1)}, f32[2]{0:T(128)}, u32[]{:S(2)}) copy-start(f32[2]{0:T(128)} %param.16) | copy-start | bytes 28
  244.9 7.7 %collective-permute-start = (bf16[2,64,256]{2,1,0:T(8,128)(2,1)S(1)}, bf16[2,64,256]{2,1,0:T(8,128)(2,1)S(1)}, u32[]{:S(2)}, u32[]{:S(2)}) collective-permute-start(bf16[2,64,256]{2,1,0:T(8,128)(2,1)S(1)} %fusion.17), channel_id=1, source_target_pairs={{0,256},{4,260},{8,264},{12,268},{16,272},{20,276},{24,280},{28,28... | collective-permute-start | bytes 196616 | tf_op jit(solution)/shard_map/ppermute | solution.py:45
  253.5 9.9 %all-to-all-start.3 = ((bf16[4,2,4096]{2,1,0:T(2,128)(2,1)}), bf16[4,2,4096]{2,1,0:T(2,128)(2,1)S(1)}, u32[]{:S(2)}, u32[]{:S(2)}) async-start(bf16[4,2,4096]{2,1,0:T(2,128)(2,1)} %reshape.152), calls=%async_computation.3 | async-start | bytes 131072 | tf_op jit(solution)/shard_map/all_to_all | solution.py:121
Sparse Core Ops, SparseCore 0:
  109.9 68.3 all-gather.5
  180.4 26.7 all-gather.7
where the time goes:
time: 274 us; the launch traced here: 273 us
  waiting for transfers between devices  114 us (42%)
  blocking collectives  77.8 us (28%)
  local copies, waits for them, and re-layouts  31.5 us (11%)
  starting transfers between devices  15.4 us (6%)
  between operations  13.6 us (5%)
  other arithmetic  11 us (4%)
  matrix products  9.71 us (4%)
    all_gather x2, waiting for transfers between devices, stacked_from(): tiles = lax.all_gather(tiles, axes[k])  82.6 us
    all_to_all x1, blocking collectives, body(): lax.all_to_all(outgoing, PAIRS, split_axis=0, concat_axis=0, tiled=True)  42.1 us
    all_to_all x1, waiting for transfers between devices, body(): lax.all_to_all(product, PAIRS, split_axis=0, concat_axis=0, tiled=True)  22.7 us
    all_gather x1, blocking collectives, body(): amp_full = lax.all_gather(amp_half, 'ints', axis=1, tiled=True)  12.6 us
    all_gather x1, blocking collectives, stacked_from(): tiles = lax.all_gather(tiles, axes[k])  12.2 us
    all_to_all x1, blocking collectives, sum_at_owner(): lax.all_to_all(tiles, axis, split_axis=0, concat_axis=0, tiled=True)  11 us
    gather x2, local copies, waits for them, and re-layouts, cycle_one(): amp_full[amp_index]  9.71 us
    dot_general x2, matrix products, cycle_one(): jnp.einsum('kac,kcb->ab', w_req, amp_full[amp_index], preferred_element_t...  9.23 us
  transfers between devices with their start and end apart: 5, of which 5 were waited for; matrix products, arithmetic and copies ran while one was open for 1% of the time, Pallas kernels for 0%

commit v1 on v0

--- a/solution.py
+++ b/solution.py
@@ -6,6 +6,13 @@
 
 PAIRS = ("pairs_0", "pairs_1", "pairs_2")
 PAIRS_INTS = ("pairs_0", "pairs_1", "pairs_2", "ints")
+
+
+def swapped_in(x, axis, along):
+    size = lax.axis_size(axis)
+    parts = jnp.stack([x for _ in range(size)])
+    parts = lax.all_to_all(parts, axis, split_axis=0, concat_axis=0)
+    return jnp.concatenate(parts, axis=along)
 
 
 def in_blocks(array, dim, size):
@@ -92,7 +99,7 @@
     x_rows = x_rows.reshape(pair_count, row_count, domain)
     partial_value = jnp.einsum("pac,pad->pcd", amp_half, x_rows, preferred_element_type=jnp.float32)
     intermed = sum_at_owner(partial_value.astype(jnp.bfloat16), "ints", 1).astype(jnp.bfloat16)
-    amp_full = lax.all_gather(amp_half, "ints", axis=1, tiled=True)
+    amp_full = swapped_in(amp_half, "ints", 1)
     owners = share_owner[:, 0]
     wanted = share_pair[:, 0]
     n_req = owners.shape[0]

time: 274 us -> 274 us (level)
  blocking collectives: 77.8 us -> 65.2 us
  waiting for transfers between devices: 114 us -> 122 us
  starting transfers between devices: 15.4 us -> 19.6 us
    all_gather x1 -> x0, blocking collectives: 12.6 us -> none  [body(): amp_full = lax.all_gather(amp_half, 'ints', axis=1, tiled=True)]
    all_to_all x0 -> x1, waiting for transfers between devices: none -> 4.51 us  [swapped_in(): parts = lax.all_to_all(parts, axis, split_axis=0, concat_axis=0)]
    all_to_all x0 -> x1, starting transfers between devices: none -> 4.28 us  [swapped_in(): parts = lax.all_to_all(parts, axis, split_axis=0, concat_axis=0)]
    all_gather x2, waiting for transfers between devices: 82.6 us -> 85.6 us  [stacked_from(): tiles = lax.all_gather(tiles, axes[k])]
  transfers between devices with their start and end apart: 5 -> 6, of which waited for: 5 -> 6; matrix products, arithmetic and copies ran while one was open for 1% -> 1% of each run, Pallas kernels for 0% -> 0%
where the time goes in v1:
time: 274 us; the launch traced here: 273 us
  waiting for transfers between devices  122 us (45%)
  blocking collectives  65.2 us (24%)
  local copies, waits for them, and re-layouts  32.2 us (12%)
  starting transfers between devices  19.6 us (7%)
  between operations  13.6 us (5%)
  other arithmetic  11.1 us (4%)
  matrix products  9.72 us (4%)
    all_gather x2, waiting for transfers between devices, stacked_from(): tiles = lax.all_gather(tiles, axes[k])  85.6 us
    all_to_all x1, blocking collectives, body(): lax.all_to_all(outgoing, PAIRS, split_axis=0, concat_axis=0, tiled=True)  42.1 us
    all_to_all x1, waiting for transfers between devices, body(): lax.all_to_all(product, PAIRS, split_axis=0, concat_axis=0, tiled=True)  22.7 us
    all_gather x1, blocking collectives, stacked_from(): tiles = lax.all_gather(tiles, axes[k])  12.2 us
    all_to_all x1, blocking collectives, sum_at_owner(): lax.all_to_all(tiles, axis, split_axis=0, concat_axis=0, tiled=True)  11 us
    gather x2, local copies, waits for them, and re-layouts, cycle_one(): amp_full[amp_index]  9.69 us
    dot_general x2, matrix products, cycle_one(): jnp.einsum('kac,kcb->ab', w_req, amp_full[amp_index], preferred_element_t...  9.23 us
    transpose x1, local copies, waits for them, and re-layouts, stacked_from(): tiles = tiles.transpose(*back, *range(len(axes), tiles.ndim))  8.27 us
  transfers between devices with their start and end apart: 6, of which 6 were waited for; matrix products, arithmetic and copies ran while one was open for 1% of the time, Pallas kernels for 0%

profile of v1, /device:TPU:2, one launch (start us, length us, event | category | flops | bytes accessed | tf_op | source)
XLA Modules:
  0.0 273.0 jit_solution(12679372218641172761)
XLA Ops:
  10.0 2.4 scatter_fusion
  12.4 42.1 %all_to_all.29 = bf16[128,2,2,256]{3,2,1,0:T(2,128)(2,1)S(1)} all-to-all(bf16[128,2,2,256]{3,2,1,0:T(2,128)(2,1)S(1)} %bitcast.83), channel_id=1, replica_groups=mesh['pairs_0'=4,'pairs_1'=16,'pairs_2'=2,'ints'=4] {'pairs_0','pairs_1'..., dimensions={0} | all-to-all | bytes 524288 | tf_op jit(solution)/shard_map/all_to_all | solution.py:93
  55.6 7.1 %all-to-all-start.1 = ((bf16[128,2,2,256]{3,2,1,0:T(2,128)(2,1)}), bf16[128,2,2,256]{3,2,1,0:T(2,128)(2,1)S(1)}, u32[]{:S(2)}, u32[]{:S(2)}) async-start(bf16[128,2,2,256]{3,2,1,0:T(2,128)(2,1)} %reshape.93), calls=%async_computation.1 | async-start | bytes 524288 | tf_op jit(solution)/shard_map/all_to_all | solution.py:97
  62.8 22.7 %all-to-all-done.1 = bf16[128,2,2,256]{3,2,1,0:T(2,128)(2,1)S(1)} async-done(((bf16[128,2,2,256]{3,2,1,0:T(2,128)(2,1)}), bf16[128,2,2,256]{3,2,1,0:T(2,128)(2,1)S(1)}, u32[]{:S(2)}, u32[]{:S(2)}) %all-to-all-start.1) | async-done | bytes 262176 | tf_op jit(solution)/shard_map/all_to_all | solution.py:97
  86.6 11.0 %all_to_all.30 = bf16[4,2,64,256]{3,2,1,0:T(8,128)(2,1)S(1)} all-to-all(bf16[4,2,64,256]{3,2,1,0:T(8,128)(2,1)S(1)} %bitcast.87), channel_id=1, replica_groups=mesh['pairs_0'=4,'pairs_1'=16,'pairs_2'=2,'ints'=4] {'ints'}, dimensions={0} | all-to-all | bytes 524288 | tf_op jit(solution)/shard_map/all_to_all | solution.py:25
  97.6 12.2 %all-gather = bf16[8,64,256]{2,1,0:T(8,128)(2,1)} all-gather(bf16[2,64,256]{2,1,0:T(8,128)(2,1)S(1)} %reduce_sum.25), channel_id=2, replica_groups=mesh['pairs_0'=4,'pairs_1'=16,'pairs_2'=2,'ints'=4] {'pairs_0'}, dimensions={0}, use_global_device_ids=true | all-gather | bytes 327680 | tf_op jit(solution)/shard_map/all_gather | solution.py:38
  109.8 68.5 %all-gather.6.cloned.1.call-done = bf16[64,2,64,256]{3,2,1,0:T(8,128)(2,1)} async-done(((bf16[4,2,64,256]{3,2,1,0:T(8,128)(2,1)}), bf16[64,2,64,256]{3,2,1,0:T(8,128)(2,1)}) %all-gather.6.cloned.1.call-update) | async-done | bytes 4194320 | tf_op jit(solution)/shard_map/all_gather | solution.py:38
  179.0 4.3 %all-to-all-start.3 = ((bf16[4,2,64,256]{3,2,1,0:T(8,128)(2,1)}), bf16[4,2,64,256]{3,2,1,0:T(8,128)(2,1)S(1)}, u32[]{:S(2)}, u32[]{:S(2)}) async-start(bf16[4,2,64,256]{3,2,1,0:T(8,128)(2,1)} %stack.2), calls=%async_computation.3 | async-start | bytes 524288 | tf_op jit(solution)/shard_map/all_to_all | solution.py:14
  185.5 4.5 %all-to-all-done.3 = bf16[4,2,64,256]{3,2,1,0:T(8,128)(2,1)S(1)} async-done(((bf16[4,2,64,256]{3,2,1,0:T(8,128)(2,1)}), bf16[4,2,64,256]{3,2,1,0:T(8,128)(2,1)S(1)}, u32[]{:S(2)}, u32[]{:S(2)}) %all-to-all-start.3) | async-done | bytes 262176 | tf_op jit(solution)/shard_map/all_to_all | solution.py:14
  190.0 17.1 %all-gather.8.cloned.1.call-done = bf16[32,4,2,64,256]{4,3,2,1,0:T(8,128)(2,1)} async-done(((bf16[16,4,2,64,256]{4,3,2,1,0:T(8,128)(2,1)}), bf16[32,4,2,64,256]{4,3,2,1,0:T(8,128)(2,1)}) %all-gather.8.cloned.1.call-update) | async-done | bytes 8388624 | tf_op jit(solution)/shard_map/all_gather | solution.py:38
  207.2 8.3 %copy.19 = bf16[4,16,2,2,64,256]{5,4,3,2,1,0:T(8,128)(2,1)} copy(bf16[4,16,2,2,64,256]{5,4,3,0,1,2:T(8,128)(2,1)} %bitcast.81) | data formatting | bytes 16777216 | tf_op jit(solution)/shard_map/transpose | solution.py:41
  215.4 5.9 %gather_fusion.2 = bf16[96,64,256]{2,1,0:T(8,128)(2,1)} fusion(bf16[256,64,256]{2,1,0:T(8,128)(2,1)} %bitcast.79, s32[1024]{0:T(1024)S(1)} %pad_clamp_fusion.2), kind=kCustom, calls=%fused_computation.2 | custom fusion | bytes 6291840 | tf_op jit(solution)/shard_map/gather | solution.py:113
  221.3 2.2 broadcast_select_fusion
  223.5 20.3 %while.10 = (s32[]{:T(128)}, f32[2,64,256]{2,1,0:T(8,128)}, bf16[2,48,64,256]{3,2,1,0:T(8,128)(2,1)S(1)}, s32[2,48]{1,0:T(2,128)}, bf16[2,256,256]{2,1,0:T(8,128)(2,1)S(1)}, /*index=5*/s32[]{:T(128)}) while((s32[]{:T(128)}, f32[2,64,256]{2,1,0:T(8,128)}, bf16[2,48,64,256]{3,2,1,0:T(8,128)(2,1)S(1)}, s32[2,48]{1,0:T(2,128)}, ...), condition=%wide.region_5.6_spmd, body=%wide.region_4.5_spmd.sunk | while | flops 402654368 | bytes 20518728 | solution.py:123
  224.2 4.9 %gather_fusion = bf16[48,256,256]{2,1,0:T(8,128)(2,1)} fusion(bf16[2,256,256]{2,1,0:T(8,128)(2,1)S(1)} %get-tuple-element.90, s32[1024]{0:T(1024)S(1)} %pad_clamp_fusion.5), kind=kCustom, calls=%fused_computation.clone.1 | custom fusion | bytes 12583104 | tf_op jit(solution)/shard_map/while/body/eval_jaxpr/gather | solution.py:120
  229.1 4.6 %fusion.29 = f32[2,64,256]{2,1,0:T(8,128)} fusion(f32[2,64,256]{2,1,0:T(8,128)} %get-tuple-element.81, s32[]{:T(128)} %get-tuple-element.80, bf16[48,256,256]{2,1,0:T(8,128)(2,1)} %gather_fusion, bf16[2,48,64,256]{3,2,1,0:T(8,128)(2,1)S(1)} %get-tuple-element.88), kind=kOutput, calls=%fused_computation.9.clone.1 | convolution fusion | flops 402653184 | bytes 7930880 | tf_op jit(solution)/shard_map/while/body/eval_jaxpr/kac,kcb->ab/dot_general | solution.py:119
  234.4 4.8 %gather_fusion = bf16[48,256,256]{2,1,0:T(8,128)(2,1)} fusion(bf16[2,256,256]{2,1,0:T(8,128)(2,1)S(1)} %get-tuple-element.90, s32[1024]{0:T(1024)S(1)} %pad_clamp_fusion.5), kind=kCustom, calls=%fused_computation.clone.1 | custom fusion | bytes 12583104 | tf_op jit(solution)/shard_map/while/body/eval_jaxpr/gather | solution.py:120
  239.2 4.6 %fusion.29 = f32[2,64,256]{2,1,0:T(8,128)} fusion(f32[2,64,256]{2,1,0:T(8,128)} %get-tuple-element.81, s32[]{:T(128)} %get-tuple-element.80, bf16[48,256,256]{2,1,0:T(8,128)(2,1)} %gather_fusion, bf16[2,48,64,256]{3,2,1,0:T(8,128)(2,1)S(1)} %get-tuple-element.88), kind=kOutput, calls=%fused_computation.9.clone.1 | convolution fusion | flops 402653184 | bytes 7930880 | tf_op jit(solution)/shard_map/while/body/eval_jaxpr/kac,kcb->ab/dot_general | solution.py:119
  243.8 1.1 fusion.17
  244.9 3.9 %collective-permute-start = (bf16[2,64,256]{2,1,0:T(8,128)(2,1)S(1)}, bf16[2,64,256]{2,1,0:T(8,128)(2,1)S(1)}, u32[]{:S(2)}, u32[]{:S(2)}) collective-permute-start(bf16[2,64,256]{2,1,0:T(8,128)(2,1)S(1)} %fusion.17), channel_id=1, source_target_pairs={{0,256},{4,260},{8,264},{12,268},{16,272},{20,276},{24,280},{28,28... | collective-permute-start | bytes 196616 | tf_op jit(solution)/shard_map/ppermute | solution.py:52
  249.4 3.1 %collective-permute-done = bf16[2,64,256]{2,1,0:T(8,128)(2,1)S(1)} collective-permute-done((bf16[2,64,256]{2,1,0:T(8,128)(2,1)S(1)}, bf16[2,64,256]{2,1,0:T(8,128)(2,1)S(1)}, u32[]{:S(2)}, u32[]{:S(2)}) %collective-permute-start) | collective-permute-done | bytes 65568 | tf_op jit(solution)/shard_map/ppermute | solution.py:52
  253.5 4.3 %all-to-all-start.4 = ((bf16[4,2,4096]{2,1,0:T(2,128)(2,1)}), bf16[4,2,4096]{2,1,0:T(2,128)(2,1)S(1)}, u32[]{:S(2)}, u32[]{:S(2)}) async-start(bf16[4,2,4096]{2,1,0:T(2,128)(2,1)} %reshape.162), calls=%async_computation.4 | async-start | bytes 131072 | tf_op jit(solution)/shard_map/all_to_all | solution.py:128
  257.8 5.6 %all-to-all-done.4 = bf16[4,2,4096]{2,1,0:T(2,128)(2,1)S(1)} async-done(((bf16[4,2,4096]{2,1,0:T(2,128)(2,1)}), bf16[4,2,4096]{2,1,0:T(2,128)(2,1)S(1)}, u32[]{:S(2)}, u32[]{:S(2)}) %all-to-all-start.4) | async-done | bytes 65568 | tf_op jit(solution)/shard_map/all_to_all | solution.py:128
  264.4 1.7 fusion.12
  (55 shorter events, 12.6 us)
Async XLA Ops:
  6.5 48.1 %copy-start = (bf16[1,256,256]{2,1,0:T(8,128)(2,1)S(1)}, bf16[1,256,256]{2,1,0:T(8,128)(2,1)}, u32[]{:S(2)}) copy-start(bf16[1,256,256]{2,1,0:T(8,128)(2,1)} %param.14) | copy-start | bytes 393220
  55.6 29.9 %all-to-all-start.1 = ((bf16[128,2,2,256]{3,2,1,0:T(2,128)(2,1)}), bf16[128,2,2,256]{3,2,1,0:T(2,128)(2,1)S(1)}, u32[]{:S(2)}, u32[]{:S(2)}) async-start(bf16[128,2,2,256]{3,2,1,0:T(2,128)(2,1)} %reshape.93), calls=%async_computation.1 | async-start | bytes 524288 | tf_op jit(solution)/shard_map/all_to_all | solution.py:97
  62.8 115.5 %all-gather.6.cloned.1.call-start = ((), (), s32[]{:S(2)}) async-start(), calls=%async_computation.5 | async-start | bytes 4456448 | tf_op jit(solution)/shard_map/all_gather | solution.py:38
  97.5 85.8 %copy-start.4 = (s32[96,1]{0,1:T(1,128)S(1)}, s32[96,1]{0,1:T(1,128)}, u32[]{:S(2)}) copy-start(s32[96,1]{0,1:T(1,128)} %param.19) | copy-start | bytes 1156
  97.5 85.8 %copy-start.5 = (s32[96,1]{0,1:T(1,128)S(1)}, s32[96,1]{0,1:T(1,128)}, u32[]{:S(2)}) copy-start(s32[96,1]{0,1:T(1,128)} %param.18) | copy-start | bytes 1156
  97.5 86.5 %copy-start.3 = (s32[96,1]{0,1:T(1,128)S(1)}, s32[96,1]{0,1:T(1,128)}, u32[]{:S(2)}) copy-start(s32[96,1]{0,1:T(1,128)} %param.20) | copy-start | bytes 1156
  97.5 87.9 %copy-start.1 = (f32[2,256]{1,0:T(2,128)S(1)}, f32[2,256]{1,0:T(2,128)}, u32[]{:S(2)}) copy-start(f32[2,256]{1,0:T(2,128)} %param.15) | copy-start | bytes 6148
  109.8 97.4 %all-gather.8.cloned.1.call-start = ((), (), s32[]{:S(2)}) async-start(), calls=%async_computation.6 | async-start | bytes 12582912 | tf_op jit(solution)/shard_map/all_gather | solution.py:38
  179.0 11.0 %all-to-all-start.3 = ((bf16[4,2,64,256]{3,2,1,0:T(8,128)(2,1)}), bf16[4,2,64,256]{3,2,1,0:T(8,128)(2,1)S(1)}, u32[]{:S(2)}, u32[]{:S(2)}) async-start(bf16[4,2,64,256]{3,2,1,0:T(8,128)(2,1)} %stack.2), calls=%async_computation.3 | async-start | bytes 524288 | tf_op jit(solution)/shard_map/all_to_all | solution.py:14
  223.5 20.3 %copy-start.2 = (f32[2]{0:T(128)S(1)}, f32[2]{0:T(128)}, u32[]{:S(2)}) copy-start(f32[2]{0:T(128)} %param.16) | copy-start | bytes 28
  244.9 7.7 %collective-permute-start = (bf16[2,64,256]{2,1,0:T(8,128)(2,1)S(1)}, bf16[2,64,256]{2,1,0:T(8,128)(2,1)S(1)}, u32[]{:S(2)}, u32[]{:S(2)}) collective-permute-start(bf16[2,64,256]{2,1,0:T(8,128)(2,1)S(1)} %fusion.17), channel_id=1, source_target_pairs={{0,256},{4,260},{8,264},{12,268},{16,272},{20,276},{24,280},{28,28... | collective-permute-start | bytes 196616 | tf_op jit(solution)/shard_map/ppermute | solution.py:52
  253.5 9.9 %all-to-all-start.4 = ((bf16[4,2,4096]{2,1,0:T(2,128)(2,1)}), bf16[4,2,4096]{2,1,0:T(2,128)(2,1)S(1)}, u32[]{:S(2)}, u32[]{:S(2)}) async-start(bf16[4,2,4096]{2,1,0:T(2,128)(2,1)} %reshape.162), calls=%async_computation.4 | async-start | bytes 131072 | tf_op jit(solution)/shard_map/all_to_all | solution.py:128
Sparse Core Ops, SparseCore 0:
  109.9 68.3 all-gather.5
  180.4 26.7 all-gather.7
